TPU v7x, 32 devices: a whole 2x2x4 slice. The times are simulated.
32 devices in a mesh: tm: 4 (over z), space: 8 (over y, x, core).
Axes of the slice: x: 2, y: 2, z: 4, core: 2. Of those that a mesh axis runs over, the one named last changes fastest.
Arguments:
- right_side: float32 [64, 2048, 128], P('space', 'tm'), may hold values from -3 to 3
- blocks: float32 [64, 7, 128, 128], P('space'), may hold values from -0.1875 to 0.1875
- neighbors: int32 [64, 7], P('space'), may hold values from 0 to 63, as said below
- shift_rates: float32 [4], replicated, may hold values from 5 to 8
Outputs:
- correction: float32 [64, 2048, 128], P('space', 'tm')
Inputs may be any that keep to these rules, and one draw needn't show every extreme that they name: The elements form planes of 8 consecutive elements. neighbors[e, 0] = e. With q the plane of e, column 1 names an element of plane q - 1 and column 2 one of plane q + 1, cyclically over the planes; within a plane, each of these two columns names every element of the neighbouring plane exactly once. Columns 3 to 6 name elements of plane q.
All inputs are finite; a program needn't handle non-finite values.
Results may differ from a plain program's by a relative error of at most 0.0003.
Values sent between devices are 32-bit elements; how exact they have to be, the bound alone decides.
A program may use at most 128 MiB of HBM per device.

v0:
```python
import functools
import math

import jax
import jax.numpy as jnp
from jax import lax
from jax.sharding import PartitionSpec as P

SWEEPS = 4
WRAP_WEIGHT = 0.01
DIAG_WEIGHT = 6.0
BLOCK_WEIGHT = 3.0
STEP_SCALE = 0.1


def cyclic_filter(value, sigma):
    plane, steps, nodes = value.shape
    devices = lax.axis_size("tm")
    me = lax.axis_index("tm")
    rate = jnp.log1p(sigma)
    ids = jnp.arange(steps, dtype=jnp.float32)
    lag = ids[:, None] - ids[None, :]
    tri = jnp.where(lag >= 0, jnp.exp(-rate * (jnp.maximum(lag, 0.0) + 1.0)), 0.0)
    local = jnp.einsum("nm,emp->enp", tri, value, precision=lax.Precision.HIGH)
    ends = lax.all_gather(local[:, -1, :], "tm")
    total = jnp.zeros_like(local[:, -1, :])
    decay = jnp.exp(-rate * steps)
    for back in range(1, devices + 1):
        source = me - back
        wrap = jnp.where(source < 0, WRAP_WEIGHT, 1.0)
        total = total + wrap * decay ** (back - 1) * ends[(source + devices) % devices]
    start = total / (1.0 - WRAP_WEIGHT * decay ** devices)
    return local + jnp.exp(-rate * (ids + 1.0))[None, :, None] * start[:, None, :]


def per_device(right_side, blocks, neighbors, shift_rates):
    plane = right_side.shape[0]
    devices = lax.axis_size("space")
    up = [(i, (i + 1) % devices) for i in range(devices)]
    down = [(j, i) for i, j in up]
    local_index = neighbors % plane
    sigma = STEP_SCALE * shift_rates
    chain = [right_side]
    for j in range(SWEEPS - 1):
        z = chain[-1]
        before = lax.ppermute(z, "space", up)
        after = lax.ppermute(z, "space", down)
        taken = [z]
        taken.append(jnp.take(before, local_index[:, 1], axis=0))
        taken.append(jnp.take(after, local_index[:, 2], axis=0))
        taken += [jnp.take(z, local_index[:, s], axis=0) for s in range(3, 7)]
        prod = jnp.einsum(
            "esij,eslj->eli", blocks, jnp.stack(taken, 1), precision=lax.Precision.HIGH
        )
        chain.append((sigma[j] - STEP_SCALE * DIAG_WEIGHT) * z - STEP_SCALE * BLOCK_WEIGHT * prod)
    out = cyclic_filter(chain[-1], sigma[SWEEPS - 1])
    for j in reversed(range(SWEEPS - 1)):
        out = cyclic_filter(chain[j] + out, sigma[j])
    return out


def solution(mesh):
    return jax.shard_map(
        per_device,
        mesh=mesh,
        in_specs=(P("space", "tm", None), P("space", None, None, None), P("space", None), P()),
        out_specs=P("space", "tm", None),
        check_vma=False,
    )
```

profile of v0, /device:TPU:0, one launch (start us, length us, event | category | flops | bytes accessed | tf_op | source)
XLA Modules:
  0.0 320.1 jit_solution(2800671011165788323)
XLA Ops:
  0.5 2.9 collective-permute-start.1
  4.4 3.8 %gather_fusion.2 = f32[8,512,128]{2,1,0:T(8,128)} fusion(f32[8,512,128]{2,1,0:T(8,128)} %param.6, s32[1024]{0:T(1024)S(1)} %pad_clamp_fusion.3), kind=kCustom, calls=%fused_computation.2.clone | custom fusion | bytes 4194336 | tf_op jit(solution)/shard_map/jit(_take)/gather | solution.py:51
  8.1 2.0 gather_fusion.3
  10.1 2.0 gather_fusion.4
  12.2 2.0 gather_fusion.5
  15.5 1.4 bitcast_dynamic-update-slice_fusion.20
  17.0 30.3 %collective-permute-done = f32[8,512,128]{2,1,0:T(8,128)} collective-permute-done((f32[8,512,128]{2,1,0:T(8,128)}, f32[8,512,128]{2,1,0:T(8,128)}, u32[]{:S(2)}, u32[]{:S(2)}) %collective-permute-start) | collective-permute-done | bytes 2097184 | tf_op jit(solution)/shard_map/ppermute | solution.py:46
  47.3 3.6 %gather_fusion = f32[8,512,128]{2,1,0:T(8,128)} fusion(f32[8,512,128]{2,1,0:T(8,128)} %collective-permute-done, s32[1024]{0:T(1024)S(1)} %pad_clamp_fusion.5), kind=kCustom, calls=%fused_computation.clone | custom fusion | bytes 4194336 | tf_op jit(solution)/shard_map/jit(_take)/gather | solution.py:49
  50.9 3.1 bitcast_dynamic-update-slice_fusion.19
  54.0 3.6 %gather_fusion.1 = f32[8,512,128]{2,1,0:T(8,128)} fusion(f32[8,512,128]{2,1,0:T(8,128)} %collective-permute-done.1, s32[1024]{0:T(1024)S(1)} %pad_clamp_fusion.4), kind=kCustom, calls=%fused_computation.1.clone | custom fusion | bytes 4194336 | tf_op jit(solution)/shard_map/jit(_take)/gather | solution.py:50
  57.6 3.3 %bitcast_dynamic-update-slice_fusion.18 = f32[8,7,512,128]{3,2,1,0:T(8,128)} fusion(f32[8,7,512,128]{3,2,1,0:T(8,128)} %bitcast_dynamic-update-slice_fusion.19, f32[8,512,128]{2,1,0:T(8,128)} %gather_fusion.1, pred[8]{0:T(512)(128)(4,1)S(1)} %get-tuple-element.26), kind=kLoop, calls=%fused_computation.47 | loop fusion | flops 524288 | bytes 4194312
  60.9 1.6 bitcast_dynamic-update-slice_fusion.17
  63.2 1.6 bitcast_dynamic-update-slice_fusion.16
  64.8 0.8 copy-done.7
  65.6 1.6 bitcast_dynamic-update-slice_fusion.15
  67.9 1.6 bitcast_dynamic-update-slice_fusion.14
  69.5 1.2 copy-done.1
  70.7 10.7 %bitcast_dynamic-update-slice_fusion.13 = (f32[8,7,512,128]{3,2,0,1:T(8,128)}, f32[8,512,128]{2,1,0:T(8,128)}) fusion(f32[8,7,512,128]{3,2,1,0:T(8,128)} %bitcast_dynamic-update-slice_fusion.14, f32[8,7,128,128]{3,2,1,0:T(8,128)S(1)} %copy-done.1, f32[8,512,128]{2,1,0:T(8,128)S(1)} %copy-done, f32[]{:T(128)} %bitcast), kind=kOutput, calls=%fused_computation.40 | convolution fusion | flops 2820145152 | bytes 24641540 | tf_op jit(solution)/shard_map/esij,eslj->eli/dot_general | solution.py:52
  82.0 2.0 collective-permute-start.3
  84.7 3.6 %gather_fusion.8 = f32[8,512,128]{2,1,0:T(8,128)} fusion(f32[8,512,128]{2,1,0:T(8,128)} %get-tuple-element.17, s32[1024]{0:T(1024)S(1)} %pad_clamp_fusion.3), kind=kCustom, calls=%fused_computation.8.clone | custom fusion | bytes 4194336 | tf_op jit(solution)/shard_map/jit(_take)/gather | solution.py:51
  88.3 3.6 %gather_fusion.9 = f32[8,512,128]{2,1,0:T(8,128)} fusion(f32[8,512,128]{2,1,0:T(8,128)} %get-tuple-element.17, s32[1024]{0:T(1024)S(1)} %pad_clamp_fusion.2), kind=kCustom, calls=%fused_computation.9.clone | custom fusion | bytes 4194336 | tf_op jit(solution)/shard_map/jit(_take)/gather | solution.py:51
  91.9 3.6 %gather_fusion.10 = f32[8,512,128]{2,1,0:T(8,128)} fusion(f32[8,512,128]{2,1,0:T(8,128)} %get-tuple-element.17, s32[1024]{0:T(1024)S(1)} %pad_clamp_fusion.1), kind=kCustom, calls=%fused_computation.10.clone | custom fusion | bytes 4194336 | tf_op jit(solution)/shard_map/jit(_take)/gather | solution.py:51
  95.4 3.6 %gather_fusion.11 = f32[8,512,128]{2,1,0:T(8,128)} fusion(f32[8,512,128]{2,1,0:T(8,128)} %get-tuple-element.17, s32[1024]{0:T(1024)S(1)} %pad_clamp_fusion), kind=kCustom, calls=%fused_computation.11.clone | custom fusion | bytes 4194336 | tf_op jit(solution)/shard_map/jit(_take)/gather | solution.py:51
  99.0 29.0 %collective-permute-done.2 = f32[8,512,128]{2,1,0:T(8,128)} collective-permute-done((f32[8,512,128]{2,1,0:T(8,128)}, f32[8,512,128]{2,1,0:T(8,128)}, u32[]{:S(2)}, u32[]{:S(2)}) %collective-permute-start.2) | collective-permute-done | bytes 2097184 | tf_op jit(solution)/shard_map/ppermute | solution.py:46
  128.0 3.6 %gather_fusion.6 = f32[8,512,128]{2,1,0:T(8,128)} fusion(f32[8,512,128]{2,1,0:T(8,128)} %collective-permute-done.2, s32[1024]{0:T(1024)S(1)} %pad_clamp_fusion.5), kind=kCustom, calls=%fused_computation.6.clone | custom fusion | bytes 4194336 | tf_op jit(solution)/shard_map/jit(_take)/gather | solution.py:49
  131.6 3.1 bitcast_dynamic-update-slice_fusion.12
  134.7 3.6 %gather_fusion.7 = f32[8,512,128]{2,1,0:T(8,128)} fusion(f32[8,512,128]{2,1,0:T(8,128)} %collective-permute-done.3, s32[1024]{0:T(1024)S(1)} %pad_clamp_fusion.4), kind=kCustom, calls=%fused_computation.7.clone | custom fusion | bytes 4194336 | tf_op jit(solution)/shard_map/jit(_take)/gather | solution.py:50
  138.3 3.3 %bitcast_dynamic-update-slice_fusion.11 = f32[8,7,512,128]{3,2,0,1:T(8,128)} fusion(f32[8,7,512,128]{3,2,0,1:T(8,128)} %bitcast_dynamic-update-slice_fusion.12, f32[8,512,128]{2,1,0:T(8,128)} %gather_fusion.7, pred[8]{0:T(512)(128)(4,1)S(1)} %get-tuple-element.26), kind=kLoop, calls=%fused_computation.38 | loop fusion | flops 524288 | bytes 4194312
  141.6 1.6 bitcast_dynamic-update-slice_fusion.10
  143.1 0.8 copy-done.14
  143.9 1.6 bitcast_dynamic-update-slice_fusion.9
  145.5 0.8 copy-done.13
  146.3 1.6 bitcast_dynamic-update-slice_fusion.8
  148.6 1.6 bitcast_dynamic-update-slice_fusion.7
  150.2 1.2 copy-done.2
  151.4 11.0 %bitcast_dynamic-update-slice_fusion.6 = (f32[8,7,512,128]{3,2,0,1:T(8,128)}, f32[8,512,128]{2,1,0:T(8,128)}) fusion(f32[8,7,512,128]{3,2,0,1:T(8,128)} %bitcast_dynamic-update-slice_fusion.7, f32[8,7,128,128]{3,2,1,0:T(8,128)S(1)} %copy-done.2, f32[8,512,128]{2,1,0:T(8,128)} %get-tuple-element.17, f32[]{:T(128)} %bitcast.10), kind=kOutput, calls=%fused_computation.31 | convolution fusion | flops 2820145152 | bytes 24641540 | tf_op jit(solution)/shard_map/esij,eslj->eli/dot_general | solution.py:52
  162.4 2.0 collective-permute-start.4
  168.5 1.8 copy.29
  170.5 3.6 %gather_fusion.14 = f32[8,512,128]{2,1,0:T(8,128)} fusion(f32[8,512,128]{2,1,0:T(8,128)} %get-tuple-element.19, s32[1024]{0:T(1024)S(1)} %pad_clamp_fusion.3), kind=kCustom, calls=%fused_computation.14.clone | custom fusion | bytes 4194336 | tf_op jit(solution)/shard_map/jit(_take)/gather | solution.py:51
  174.1 3.6 %gather_fusion.15 = f32[8,512,128]{2,1,0:T(8,128)} fusion(f32[8,512,128]{2,1,0:T(8,128)} %get-tuple-element.19, s32[1024]{0:T(1024)S(1)} %pad_clamp_fusion.2), kind=kCustom, calls=%fused_computation.15.clone | custom fusion | bytes 4194336 | tf_op jit(solution)/shard_map/jit(_take)/gather | solution.py:51
  177.7 3.6 %gather_fusion.16 = f32[8,512,128]{2,1,0:T(8,128)} fusion(f32[8,512,128]{2,1,0:T(8,128)} %get-tuple-element.19, s32[1024]{0:T(1024)S(1)} %pad_clamp_fusion.1), kind=kCustom, calls=%fused_computation.16.clone | custom fusion | bytes 4194336 | tf_op jit(solution)/shard_map/jit(_take)/gather | solution.py:51
  181.3 2.3 gather_fusion.17
  183.6 27.3 %collective-permute-done.4 = f32[8,512,128]{2,1,0:T(8,128)} collective-permute-done((f32[8,512,128]{2,1,0:T(8,128)}, f32[8,512,128]{2,1,0:T(8,128)}, u32[]{:S(2)}, u32[]{:S(2)}) %collective-permute-start.4) | collective-permute-done | bytes 2097184 | tf_op jit(solution)/shard_map/ppermute | solution.py:46
  210.8 3.6 %gather_fusion.12 = f32[8,512,128]{2,1,0:T(8,128)} fusion(f32[8,512,128]{2,1,0:T(8,128)} %collective-permute-done.4, s32[1024]{0:T(1024)S(1)} %pad_clamp_fusion.5), kind=kCustom, calls=%fused_computation.12.clone | custom fusion | bytes 4194336 | tf_op jit(solution)/shard_map/jit(_take)/gather | solution.py:49
  214.5 3.1 bitcast_dynamic-update-slice_fusion.5
  217.6 3.6 %gather_fusion.13 = f32[8,512,128]{2,1,0:T(8,128)} fusion(f32[8,512,128]{2,1,0:T(8,128)} %collective-permute-done.5, s32[1024]{0:T(1024)S(1)} %pad_clamp_fusion.4), kind=kCustom, calls=%fused_computation.13.clone | custom fusion | bytes 4194336 | tf_op jit(solution)/shard_map/jit(_take)/gather | solution.py:50
  221.2 3.3 %bitcast_dynamic-update-slice_fusion.4 = f32[8,7,512,128]{3,2,0,1:T(8,128)} fusion(f32[8,7,512,128]{3,2,0,1:T(8,128)} %bitcast_dynamic-update-slice_fusion.5, f32[8,512,128]{2,1,0:T(8,128)} %gather_fusion.13, pred[8]{0:T(512)(128)(4,1)S(1)} %get-tuple-element.26), kind=kLoop, calls=%fused_computation.29 | loop fusion | flops 524288 | bytes 4194312
  224.5 1.6 bitcast_dynamic-update-slice_fusion.3
  226.0 0.8 copy-done.10
  226.8 1.6 bitcast_dynamic-update-slice_fusion.2
  229.2 1.6 bitcast_dynamic-update-slice_fusion.1
  230.7 1.5 bitcast_dynamic-update-slice_fusion
  232.2 1.3 copy-done.3
  233.5 9.4 %fusion = f32[8,512,128,1]{2,1,0,3:T(8,128)S(1)} fusion(f32[8,7,512,128]{3,2,0,1:T(8,128)} %bitcast_dynamic-update-slice_fusion, f32[8,7,128,128]{3,2,1,0:T(8,128)S(1)} %copy-done.3), kind=kOutput, calls=%fused_computation.18 | convolution fusion | flops 2818572288 | bytes 20447232 | tf_op jit(solution)/shard_map/esij,eslj->eli/dot_general | solution.py:52
  242.9 3.7 %fusion.33 = f32[8,512,128]{2,1,0:T(8,128)S(1)} fusion(f32[8,512,128,1]{2,1,0,3:T(8,128)S(1)} %fusion, f32[8,512,128]{2,1,0:T(8,128)} %get-tuple-element.19, f32[]{:T(128)} %bitcast.19, f32[]{:T(128)} %bitcast.28), kind=kOutput, calls=%fused_computation.67 | convolution fusion | flops 1613758464 | bytes 6291464 | tf_op jit(solution)/shard_map/nm,emp->enp/dot_general | solution.py:24
  246.6 14.9 %all-gather = f32[32,1,128]{2,1,0:T(1,128)S(1)} all-gather(f32[8,1,128]{2,1,0:T(1,128)S(1)} %slice.107), channel_id=2, replica_groups=mesh['tm'=4,'space'=8] {'tm'}, dimensions={0}, use_global_device_ids=true | all-gather | bytes 20480 | tf_op jit(solution)/shard_map/all_gather | solution.py:25
  261.5 3.8 %fusion.24 = f32[8,512,128]{2,1,0:T(8,128)S(1)} fusion(f32[8,512,128]{2,1,0:T(8,128)} %get-tuple-element.19, f32[8,512,128]{2,1,0:T(8,128)S(1)} %fusion.33, f32[8,128]{1,0:T(8,128)S(1)} %divide_bitcast_fusion.3, f32[512]{0:T(512)S(1)} %multiply_exponential_fusion.3, f32[]{:T(128)} %bitcast.33), kind=kOutput, calls=%fused_computation.64 | convolution fusion | flops 1613758464 | bytes 6297604 | tf_op jit(solution)/shard_map/nm,emp->enp/dot_general | solution.py:24
  265.3 13.4 %all-gather.1 = f32[32,1,128]{2,1,0:T(1,128)S(1)} all-gather(f32[8,1,128]{2,1,0:T(1,128)S(1)} %slice.108), channel_id=3, replica_groups=mesh['tm'=4,'space'=8] {'tm'}, dimensions={0}, use_global_device_ids=true | all-gather | bytes 20480 | tf_op jit(solution)/shard_map/all_gather | solution.py:25
  278.8 5.2 %fusion.27 = f32[8,512,128]{1,2,0:T(8,128)S(1)} fusion(f32[8,512,128]{2,1,0:T(8,128)} %get-tuple-element.17, f32[8,512,128]{2,1,0:T(8,128)S(1)} %fusion.24, f32[8,128]{1,0:T(8,128)S(1)} %divide_bitcast_fusion.2, f32[512]{0:T(512)S(1)} %multiply_exponential_fusion.2, f32[]{:T(128)} %bitcast.38), kind=kOutput, calls=%fused_computation.65 | convolution fusion | flops 1613758464 | bytes 6297604 | tf_op jit(solution)/shard_map/nm,emp->enp/dot_general | solution.py:24
  284.4 13.2 %all-gather.2 = f32[32,1,128]{2,1,0:T(1,128)S(1)} all-gather(f32[8,1,128]{2,1,0:T(1,128)S(1)} %copy.28), channel_id=4, replica_groups=mesh['tm'=4,'space'=8] {'tm'}, dimensions={0}, use_global_device_ids=true | all-gather | bytes 20480 | tf_op jit(solution)/shard_map/all_gather | solution.py:25
  297.7 4.3 %fusion.30 = f32[8,512,128]{1,2,0:T(8,128)S(1)} fusion(f32[8,512,128]{1,2,0:T(8,128)} %copy.29, f32[8,512,128]{1,2,0:T(8,128)} %copy-done.4, f32[8,128]{1,0:T(8,128)S(1)} %divide_bitcast_fusion.1, f32[512]{0:T(512)S(1)} %multiply_exponential_fusion.1, f32[]{:T(128)} %bitcast.43), kind=kOutput, calls=%fused_computation.66 | convolution fusion | flops 1613758464 | bytes 6297604 | tf_op jit(solution)/shard_map/nm,emp->enp/dot_general | solution.py:24
  302.4 13.2 %all-gather.3 = f32[32,1,128]{2,1,0:T(1,128)S(1)} all-gather(f32[8,1,128]{2,1,0:T(1,128)S(1)} %copy.30), channel_id=5, replica_groups=mesh['tm'=4,'space'=8] {'tm'}, dimensions={0}, use_global_device_ids=true | all-gather | bytes 20480 | tf_op jit(solution)/shard_map/all_gather | solution.py:25
  315.6 1.6 multiply_add_fusion
  317.2 2.9 copy.31
  (65 shorter events, 7.4 us)
Async XLA Ops:
  0.0 47.3 %collective-permute-start = (f32[8,512,128]{2,1,0:T(8,128)}, f32[8,512,128]{2,1,0:T(8,128)}, u32[]{:S(2)}, u32[]{:S(2)}) collective-permute-start(f32[8,512,128]{2,1,0:T(8,128)} %param.6), channel_id=1, source_target_pairs={{0,1},{1,2},{2,3},{3,4},{4,5},{5,6},{6,7},{7,0},{8,9},{9,10},{10,1... | collective-permute-start | bytes 6291464 | tf_op jit(solution)/shard_map/ppermute | solution.py:46
  0.5 53.5 %collective-permute-start.1 = (f32[8,512,128]{2,1,0:T(8,128)}, f32[8,512,128]{2,1,0:T(8,128)}, u32[]{:S(2)}, u32[]{:S(2)}) collective-permute-start(f32[8,512,128]{2,1,0:T(8,128)} %param.6), channel_id=1, source_target_pairs={{1,0},{2,1},{3,2},{4,3},{5,4},{6,5},{7,6},{0,7},{9,8},{10,9},{11,1... | collective-permute-start | bytes 6291464 | tf_op jit(solution)/shard_map/ppermute | solution.py:47
  4.4 3.8 %copy-start = (f32[8,512,128]{2,1,0:T(8,128)S(1)}, f32[8,512,128]{2,1,0:T(8,128)}, u32[]{:S(2)}) copy-start(f32[8,512,128]{2,1,0:T(8,128)} %param.6) | copy-start | bytes 6291460
  12.1 2.0 copy-start.16
  57.6 3.3 %copy-start.5 = (f32[8,512,128]{2,1,0:T(8,128)S(1)}, f32[8,512,128]{2,1,0:T(8,128)}, u32[]{:S(2)}) copy-start(f32[8,512,128]{2,1,0:T(8,128)} %gather_fusion.2) | copy-start | bytes 6291460
  60.9 2.3 copy-start.6
  63.2 2.3 copy-start.7
  65.6 2.3 copy-start.8
  67.9 2.8 copy-start.1
  81.4 46.6 %collective-permute-start.2 = (f32[8,512,128]{2,1,0:T(8,128)}, f32[8,512,128]{2,1,0:T(8,128)}, u32[]{:S(2)}, u32[]{:S(2)}) collective-permute-start(f32[8,512,128]{2,1,0:T(8,128)} %get-tuple-element.17), channel_id=1, source_target_pairs={{0,1},{1,2},{2,3},{3,4},{4,5},{5,6},{6,7},{7,0},{8,9},{9,10},{10,1... | collective-permute-start | bytes 6291464 | tf_op jit(solution)/shard_map/ppermute | solution.py:46
  82.0 52.7 %collective-permute-start.3 = (f32[8,512,128]{2,1,0:T(8,128)}, f32[8,512,128]{2,1,0:T(8,128)}, u32[]{:S(2)}, u32[]{:S(2)}) collective-permute-start(f32[8,512,128]{2,1,0:T(8,128)} %get-tuple-element.17), channel_id=1, source_target_pairs={{1,0},{2,1},{3,2},{4,3},{5,4},{6,5},{7,6},{0,7},{9,8},{10,9},{11,1... | collective-permute-start | bytes 6291464 | tf_op jit(solution)/shard_map/ppermute | solution.py:47
  138.3 3.3 %copy-start.15 = (f32[8,512,128]{2,1,0:T(8,128)S(1)}, f32[8,512,128]{2,1,0:T(8,128)}, u32[]{:S(2)}) copy-start(f32[8,512,128]{2,1,0:T(8,128)} %gather_fusion.8) | copy-start | bytes 6291460
  141.6 2.3 copy-start.14
  143.9 2.3 copy-start.13
  146.3 2.3 copy-start.12
  148.6 2.8 copy-start.2
  162.4 48.4 %collective-permute-start.4 = (f32[8,512,128]{2,1,0:T(8,128)}, f32[8,512,128]{2,1,0:T(8,128)}, u32[]{:S(2)}, u32[]{:S(2)}) collective-permute-start(f32[8,512,128]{2,1,0:T(8,128)} %get-tuple-element.19), channel_id=1, source_target_pairs={{0,1},{1,2},{2,3},{3,4},{4,5},{5,6},{6,7},{7,0},{8,9},{9,10},{10,1... | collective-permute-start | bytes 6291464 | tf_op jit(solution)/shard_map/ppermute | solution.py:46
  164.4 53.1 %collective-permute-start.5 = (f32[8,512,128]{2,1,0:T(8,128)}, f32[8,512,128]{2,1,0:T(8,128)}, u32[]{:S(2)}, u32[]{:S(2)}) collective-permute-start(f32[8,512,128]{2,1,0:T(8,128)} %get-tuple-element.19), channel_id=1, source_target_pairs={{1,0},{2,1},{3,2},{4,3},{5,4},{6,5},{7,6},{0,7},{9,8},{10,9},{11,1... | collective-permute-start | bytes 6291464 | tf_op jit(solution)/shard_map/ppermute | solution.py:47
  221.2 3.3 %copy-start.11 = (f32[8,512,128]{2,1,0:T(8,128)S(1)}, f32[8,512,128]{2,1,0:T(8,128)}, u32[]{:S(2)}) copy-start(f32[8,512,128]{2,1,0:T(8,128)} %gather_fusion.14) | copy-start | bytes 6291460
  224.5 2.3 copy-start.10
  226.8 2.3 copy-start.9
  230.7 2.8 copy-start.3
  284.0 13.6 %copy-start.4 = (f32[8,512,128]{1,2,0:T(8,128)}, f32[8,512,128]{1,2,0:T(8,128)S(1)}, u32[]{:S(2)}) copy-start(f32[8,512,128]{1,2,0:T(8,128)S(1)} %fusion.27) | copy-start | bytes 6291460
where the time goes:
time: 323 us; the launch traced here: 320 us
  waiting for transfers between devices  86.5 us (27%)
  local copies, waits for them, and re-layouts  76.5 us (24%)
  blocking collectives  54.7 us (17%)
  matrix products  48.2 us (15%)
  other arithmetic  40.5 us (13%)
  starting transfers between devices  8.65 us (3%)
  between operations  4.99 us (2%)
    ppermute x3, waiting for transfers between devices, per_device(): before = lax.ppermute(z, 'space', up)  86.5 us
    all_gather x4, blocking collectives, cyclic_filter(): ends = lax.all_gather(local[:, -1, :], 'tm')  54.7 us
    gather x12, local copies, waits for them, and re-layouts, per_device(): taken += [jnp.take(z, local_index[:, s], axis=0) for s in range(3, 7)]  37.2 us
    unnamed x15, other arithmetic  33.4 us
    dot_general x3, matrix products, per_device(): jnp.einsum('esij,eslj->eli', blocks, jnp.stack(taken, 1), precision=lax.P...  31.1 us
    dot_general x4, matrix products, cyclic_filter(): local = jnp.einsum('nm,emp->enp', tri, value, precision=lax.Precision.HIGH)  17.1 us
    unnamed x36, local copies, waits for them, and re-layouts  13.1 us
    gather x3, local copies, waits for them, and re-layouts, per_device(): taken.append(jnp.take(before, local_index[:, 1], axis=0))  10.8 us
  transfers between devices with their start and end apart: 6, of which 3 were waited for; matrix products, arithmetic and copies ran while one was open for 19% of the time, Pallas kernels for 0%

commit v1 on v0

v1 whole, which is shorter than its diff:
```python
import functools
import math

import jax
import jax.numpy as jnp
from jax import lax
from jax.experimental import pallas as pl
from jax.experimental.pallas import tpu as pltpu
from jax.sharding import PartitionSpec as P

SWEEPS = 4
SLOTS = 7
CHUNKS = 4
ROWS = 8
WRAP_WEIGHT = 0.01
DIAG_WEIGHT = 6.0
BLOCK_WEIGHT = 3.0
STEP_SCALE = 0.1
MESH = pl.DeviceIdType.MESH


def split(value):
    hi = value.astype(jnp.bfloat16)
    lo = (value - hi.astype(jnp.float32)).astype(jnp.bfloat16)
    return hi, lo


def kernel(tm_size, sp_size, x_ref, blocks_ref, local_ref, coef_ref, out_ref, *scratch):
    plane, steps, nodes = x_ref.shape
    width = steps // CHUNKS
    moves = SWEEPS - 1
    zs = [x_ref] + list(scratch[:moves])
    halos = scratch[moves : moves + 2 * moves * CHUNKS]
    weights, table, gathered, own, send_sem, recv_sem, end_send, end_recv = scratch[
        moves + 2 * moves * CHUNKS :
    ]
    tm = lax.axis_index("tm")
    sp = lax.axis_index("space")
    sides = (lax.rem(sp + 1, sp_size), lax.rem(sp + sp_size - 1, sp_size))
    peers = [lax.rem(tm + r, tm_size) for r in range(1, tm_size)]

    barrier = pltpu.get_barrier_semaphore()
    for side in sides:
        pl.semaphore_signal(barrier, inc=1, device_id={"space": side}, device_id_type=MESH)
    for peer in peers:
        pl.semaphore_signal(barrier, inc=1, device_id={"tm": peer}, device_id_type=MESH)
    pl.semaphore_wait(barrier, 2 + len(peers))

    def halo(j, c, d):
        return halos[(j * CHUNKS + c) * 2 + d]

    def transfer(j, c, d):
        return pltpu.make_async_remote_copy(
            src_ref=zs[j].at[:, pl.ds(c * width, width), :],
            dst_ref=halo(j, c, d),
            send_sem=send_sem.at[j, c, d],
            recv_sem=recv_sem.at[j, c, d],
            device_id={"space": sides[d]},
            device_id_type=MESH,
        )

    for c in range(CHUNKS):
        for d in range(2):
            transfer(0, c, d).start()

    def prepare(e, _):
        for s in range(SLOTS):
            hi, lo = split((-STEP_SCALE * BLOCK_WEIGHT) * blocks_ref[e, s].T)
            weights[e, s * nodes : (s + 1) * nodes, :nodes] = hi
            weights[e, s * nodes : (s + 1) * nodes, nodes:] = lo
        return 0

    lax.fori_loop(0, plane, prepare, 0)

    rates = [coef_ref[i] for i in range(SWEEPS)]

    def cascade(inputs, states):
        states = list(states)
        above = None
        for i in reversed(range(SWEEPS)):
            total = states[i] if inputs is None else inputs[i] + states[i]
            if above is not None:
                total = total + above
            states[i] = above = rates[i] * total
        return states

    row = lax.broadcasted_iota(jnp.int32, (ROWS, nodes), 0)
    unit = [(row == i).astype(jnp.float32) for i in range(SWEEPS)]

    def respond(g, states):
        kept = []
        for _ in range(ROWS):
            states = cascade(None, states)
            kept.append(states[0])
        flat = jnp.swapaxes(jnp.stack(kept), 0, 1)
        base = pl.multiple_of(g * ROWS, ROWS)
        for j in range(SWEEPS):
            table[j, pl.ds(base, ROWS), :] = flat[j]
        return tuple(states)

    over = lax.fori_loop(0, steps // ROWS, respond, tuple(unit))
    carry_of = [[over[i][j : j + 1, :] for j in range(SWEEPS)] for i in range(SWEEPS)]

    def advance(vectors):
        result = []
        for i in range(SWEEPS):
            total = carry_of[i][i] * vectors[i]
            for j in range(i + 1, SWEEPS):
                total = total + carry_of[i][j] * vectors[j]
            result.append(total)
        return result

    around = list(over)
    for _ in range(tm_size - 1):
        around = advance(around)

    states = tuple(jnp.zeros((ROWS, nodes), jnp.float32) for _ in range(SWEEPS))
    for j in range(moves):
        diag = coef_ref[SWEEPS + j]
        for c in range(CHUNKS):
            for d in range(2):
                transfer(j, c, d).wait_recv()
            window = pl.ds(c * width, width)

            def apply(e, _):
                here = zs[j][e, window, :]
                parts = [
                    here,
                    halo(j, c, 0)[local_ref[e, 1]],
                    halo(j, c, 1)[local_ref[e, 2]],
                ] + [zs[j][local_ref[e, s], window, :] for s in range(3, SLOTS)]
                pairs = [split(part) for part in parts]
                hi = jnp.concatenate([p[0] for p in pairs], axis=1)
                lo = jnp.concatenate([p[1] for p in pairs], axis=1)
                both = jnp.dot(hi, weights[e], preferred_element_type=jnp.float32)
                both = both + jnp.dot(lo, weights[e], preferred_element_type=jnp.float32)
                zs[j + 1][e, window, :] = diag * here + both[:, :nodes] + both[:, nodes:]
                return 0

            lax.fori_loop(0, plane, apply, 0)
            if j + 1 < moves:
                for d in range(2):
                    transfer(j + 1, c, d).start()
            else:

                def scan(g, states):
                    base = pl.multiple_of(c * width + g * ROWS, ROWS)
                    here = [jnp.swapaxes(z[:, pl.ds(base, ROWS), :], 0, 1) for z in zs]
                    kept = []
                    for t in range(ROWS):
                        states = cascade([h[t] for h in here], states)
                        kept.append(states[0])
                    out_ref[:, pl.ds(base, ROWS), :] = jnp.swapaxes(jnp.stack(kept), 0, 1)
                    return tuple(states)

                states = lax.fori_loop(0, width // ROWS, scan, states)

    for i in range(SWEEPS):
        own[i] = states[i]
    ends = [
        pltpu.make_async_remote_copy(
            src_ref=own,
            dst_ref=gathered.at[r],
            send_sem=end_send.at[r],
            recv_sem=end_recv.at[r],
            device_id={"tm": peers[r]},
            device_id_type=MESH,
        )
        for r in range(tm_size - 1)
    ]
    for copy in ends:
        copy.start()
    for copy in ends:
        copy.wait()

    def enter(back):
        entered = lax.rem(tm - back + 1 + tm_size, tm_size)
        return jnp.where(entered == 0, jnp.float32(WRAP_WEIGHT), jnp.float32(1.0))

    total = [enter(tm_size) * own[i] for i in range(SWEEPS)]
    for back in range(tm_size - 1, 0, -1):
        moved = advance(total)
        total = [enter(back) * (gathered[back - 1, i] + moved[i]) for i in range(SWEEPS)]
    start = [None] * SWEEPS
    for i in reversed(range(SWEEPS)):
        value = total[i]
        for j in range(i + 1, SWEEPS):
            value = value + WRAP_WEIGHT * around[i][j : j + 1, :] * start[j]
        start[i] = value / (1.0 - WRAP_WEIGHT * around[i][i : i + 1, :])
    for e in range(plane):
        value = out_ref[e]
        for i in range(SWEEPS):
            value = value + table[i] * start[i][e : e + 1, :]
        out_ref[e] = value

    for j in range(moves):
        for c in range(CHUNKS):
            for d in range(2):
                transfer(j, c, d).wait_send()


def solution(mesh):
    tm_size, sp_size = mesh.shape["tm"], mesh.shape["space"]

    def per_device(right_side, blocks, neighbors, shift_rates):
        plane, steps, nodes = right_side.shape
        moves = SWEEPS - 1
        sigma = STEP_SCALE * shift_rates
        coef = jnp.concatenate([1.0 / (1.0 + sigma), sigma - STEP_SCALE * DIAG_WEIGHT])
        whole = pltpu.VMEM((plane, steps, nodes), jnp.float32)
        piece = pltpu.VMEM((plane, steps // CHUNKS, nodes), jnp.float32)
        dma = pltpu.SemaphoreType.DMA
        return pl.pallas_call(
            functools.partial(kernel, tm_size, sp_size),
            out_shape=jax.ShapeDtypeStruct(right_side.shape, jnp.float32),
            in_specs=[
                pl.BlockSpec(memory_space=pltpu.VMEM),
                pl.BlockSpec(memory_space=pltpu.VMEM),
                pl.BlockSpec(memory_space=pltpu.SMEM),
                pl.BlockSpec(memory_space=pltpu.SMEM),
            ],
            out_specs=pl.BlockSpec(memory_space=pltpu.VMEM),
            scratch_shapes=[whole] * moves
            + [piece] * (2 * moves * CHUNKS)
            + [
                pltpu.VMEM((plane, SLOTS * nodes, 2 * nodes), jnp.bfloat16),
                pltpu.VMEM((SWEEPS, steps, nodes), jnp.float32),
                pltpu.VMEM((tm_size - 1, SWEEPS, plane, nodes), jnp.float32),
                pltpu.VMEM((SWEEPS, plane, nodes), jnp.float32),
                dma((moves, CHUNKS, 2)),
                dma((moves, CHUNKS, 2)),
                dma((tm_size - 1,)),
                dma((tm_size - 1,)),
            ],
            compiler_params=pltpu.CompilerParams(
                collective_id=0, has_side_effects=True, vmem_limit_bytes=56 * 2**20
            ),
        )(right_side, blocks, neighbors % plane, coef)

    return jax.shard_map(
        per_device,
        mesh=mesh,
        in_specs=(P("space", "tm", None), P("space", None, None, None), P("space", None), P()),
        out_specs=P("space", "tm", None),
        check_vma=False,
    )
```

time: 323 us -> 159 us (0.49)
  Pallas kernels: 0 us -> 153 us
  waiting for transfers between devices: 86.5 us -> 0 us
  local copies, waits for them, and re-layouts: 76.5 us -> 3.06 us
  blocking collectives: 54.7 us -> 0 us
  matrix products: 48.2 us -> 0 us
  other arithmetic: 40.5 us -> 2.57 us
  starting transfers between devices: 8.65 us -> 0 us
  between operations: 4.99 us -> 0.01 us
    pallas_call x0 -> x1, Pallas kernels: none -> 153 us  [per_device(): pl.pallas_call(functools.partial(kernel, tm_size, sp_size), out_shape=jax...]
    ppermute x6 -> x0, waiting for transfers between devices: 86.5 us -> none  [the longest x3 86.5 us: per_device(): before = lax.ppermute(z, 'space', up)]
    gather x18 -> x0, local copies, waits for them, and re-layouts: 58.8 us -> none  [the longest x12 37.2 us: per_device(): taken += [jnp.take(z, local_index[:, s], axis=0) for s in range(3, 7)]]
    all_gather x4 -> x0, blocking collectives: 54.7 us -> none  [cyclic_filter(): ends = lax.all_gather(local[:, -1, :], 'tm')]
    dot_general x7 -> x0, matrix products: 48.2 us -> none  [the longest x3 31.1 us: per_device(): jnp.einsum('esij,eslj->eli', blocks, jnp.stack(taken, 1), precision=lax.P...]
    unnamed x15 -> x0, other arithmetic: 33.4 us -> none
    unnamed x36 -> x1, local copies, waits for them, and re-layouts: 13.1 us -> 3.06 us
    ppermute x6 -> x0, starting transfers between devices: 8.65 us -> none  [the longest x3 5.53 us: per_device(): after = lax.ppermute(z, 'space', down)]
  transfers between devices with their start and end apart: 6 -> 0, of which waited for: 3 -> 0; matrix products, arithmetic and copies ran while one was open for 19% -> 0% of each run, Pallas kernels for 0% -> 0%
where the time goes in v1:
time: 159 us
  Pallas kernels  153 us (96%)
  local copies, waits for them, and re-layouts  3.06 us (2%)
  other arithmetic  2.57 us (2%)
    pallas_call x1, Pallas kernels, per_device(): pl.pallas_call(functools.partial(kernel, tm_size, sp_size), out_shape=jax...  153 us

profile of v1, /device:TPU:0, one launch (start us, length us, event | category | flops | bytes accessed | tf_op | source)
XLA Modules:
  0.0 159.1 jit_solution(10794563103061863888)
XLA Ops:
  0.0 0.7 add_divide_fusion
  0.7 0.6 pad_maximum_fusion.coef_ref
  1.3 1.3 add_select_fusion.local_ref
  2.6 153.4 %shard_map.46 = f32[8,512,128]{2,1,0:T(8,128)} custom-call(f32[8,512,128]{2,1,0:T(8,128)} %x_ref.1, f32[8,7,128,128]{3,2,1,0:T(8,128)} %blocks_ref.1, s32[8,7]{1,0:T(8,128)} %add_select_fusion.local_ref, f32[8]{0:T(128)} %pad_maximum_fusion.coef_ref), custom_call_target="tpu_custom_call" | custom-call | tf_op jit(solution)/shard_map/pallas_call | solution.py:213
  156.0 3.1 %copy.6 = f32[8,512,128]{2,1,0:T(8,128)} copy(f32[8,512,128]{2,1,0:T(8,128)} %shard_map.46) | data formatting | bytes 4194304

commit v2 on v1

--- a/solution.py
+++ b/solution.py
@@ -10,7 +10,8 @@
 
 SWEEPS = 4
 SLOTS = 7
-CHUNKS = 4
+PIECES = (4, 4, 4, 2, 1, 1)
+CHUNKS = len(PIECES)
 ROWS = 8
 WRAP_WEIGHT = 0.01
 DIAG_WEIGHT = 6.0
@@ -25,14 +26,23 @@
     return hi, lo
 
 
-def kernel(tm_size, sp_size, x_ref, blocks_ref, local_ref, coef_ref, out_ref, *scratch):
+def windows(steps):
+    unit = steps // sum(PIECES)
+    return [(unit * sum(PIECES[:c]), unit * PIECES[c]) for c in range(CHUNKS)]
+
+
+def kernel(
+    tm_size, sp_size, x_ref, blocks_ref, near_ref, shift_ref,
+    series_ref, table_ref, start_ref, *scratch
+):
     plane, steps, nodes = x_ref.shape
-    width = steps // CHUNKS
+    spans = windows(steps)
     moves = SWEEPS - 1
-    zs = [x_ref] + list(scratch[:moves])
-    halos = scratch[moves : moves + 2 * moves * CHUNKS]
-    weights, table, gathered, own, send_sem, recv_sem, end_send, end_recv = scratch[
-        moves + 2 * moves * CHUNKS :
+    zs = list(scratch[:SWEEPS])
+    halos = scratch[SWEEPS : SWEEPS + 2 * moves * CHUNKS]
+    (series, held, weights, table, gathered, own,
+     send_sem, recv_sem, end_send, end_recv, load_sem, store_sem) = scratch[
+        SWEEPS + 2 * moves * CHUNKS :
     ]
     tm = lax.axis_index("tm")
     sp = lax.axis_index("space")
@@ -44,14 +54,21 @@
         pl.semaphore_signal(barrier, inc=1, device_id={"space": side}, device_id_type=MESH)
     for peer in peers:
         pl.semaphore_signal(barrier, inc=1, device_id={"tm": peer}, device_id_type=MESH)
+    load_blocks = pltpu.make_async_copy(blocks_ref, held, load_sem.at[0])
+    load_x = pltpu.make_async_copy(x_ref, zs[0], load_sem.at[1])
+    load_blocks.start()
+    load_x.start()
     pl.semaphore_wait(barrier, 2 + len(peers))
+
+    def near(e, s):
+        return lax.rem(near_ref[e, s], plane)
 
     def halo(j, c, d):
         return halos[(j * CHUNKS + c) * 2 + d]
 
     def transfer(j, c, d):
         return pltpu.make_async_remote_copy(
-            src_ref=zs[j].at[:, pl.ds(c * width, width), :],
+            src_ref=(x_ref if j == 0 else zs[j]).at[:, pl.ds(*spans[c]), :],
             dst_ref=halo(j, c, d),
             send_sem=send_sem.at[j, c, d],
             recv_sem=recv_sem.at[j, c, d],
@@ -63,16 +80,19 @@
         for d in range(2):
             transfer(0, c, d).start()
 
+    load_blocks.wait()
+
     def prepare(e, _):
         for s in range(SLOTS):
-            hi, lo = split((-STEP_SCALE * BLOCK_WEIGHT) * blocks_ref[e, s].T)
+            hi, lo = split((-STEP_SCALE * BLOCK_WEIGHT) * held[e, s].T)
             weights[e, s * nodes : (s + 1) * nodes, :nodes] = hi
             weights[e, s * nodes : (s + 1) * nodes, nodes:] = lo
         return 0
 
     lax.fori_loop(0, plane, prepare, 0)
 
-    rates = [coef_ref[i] for i in range(SWEEPS)]
+    sigmas = [STEP_SCALE * shift_ref[i] for i in range(SWEEPS)]
+    rates = [1.0 / (1.0 + jnp.full((ROWS, nodes), sigma, jnp.float32)) for sigma in sigmas]
 
     def cascade(inputs, states):
         states = list(states)
@@ -99,6 +119,8 @@
         return tuple(states)
 
     over = lax.fori_loop(0, steps // ROWS, respond, tuple(unit))
+    save_table = pltpu.make_async_copy(table, table_ref, store_sem.at[CHUNKS])
+    save_table.start()
     carry_of = [[over[i][j : j + 1, :] for j in range(SWEEPS)] for i in range(SWEEPS)]
 
     def advance(vectors):
@@ -114,21 +136,29 @@
     for _ in range(tm_size - 1):
         around = advance(around)
 
+    load_x.wait()
+    def save(c):
+        window = pl.ds(*spans[c])
+        return pltpu.make_async_copy(
+            series.at[:, window, :], series_ref.at[:, window, :], store_sem.at[c]
+        )
+
     states = tuple(jnp.zeros((ROWS, nodes), jnp.float32) for _ in range(SWEEPS))
     for j in range(moves):
-        diag = coef_ref[SWEEPS + j]
+        diag = sigmas[j] - STEP_SCALE * DIAG_WEIGHT
         for c in range(CHUNKS):
             for d in range(2):
                 transfer(j, c, d).wait_recv()
-            window = pl.ds(c * width, width)
+            first, width = spans[c]
+            window = pl.ds(first, width)
 
             def apply(e, _):
                 here = zs[j][e, window, :]
                 parts = [
                     here,
-                    halo(j, c, 0)[local_ref[e, 1]],
-                    halo(j, c, 1)[local_ref[e, 2]],
-                ] + [zs[j][local_ref[e, s], window, :] for s in range(3, SLOTS)]
+                    halo(j, c, 0)[near(e, 1)],
+                    halo(j, c, 1)[near(e, 2)],
+                ] + [zs[j][near(e, s), window, :] for s in range(3, SLOTS)]
                 pairs = [split(part) for part in parts]
                 hi = jnp.concatenate([p[0] for p in pairs], axis=1)
                 lo = jnp.concatenate([p[1] for p in pairs], axis=1)
@@ -144,16 +174,17 @@
             else:
 
                 def scan(g, states):
-                    base = pl.multiple_of(c * width + g * ROWS, ROWS)
+                    base = pl.multiple_of(first + g * ROWS, ROWS)
                     here = [jnp.swapaxes(z[:, pl.ds(base, ROWS), :], 0, 1) for z in zs]
                     kept = []
                     for t in range(ROWS):
                         states = cascade([h[t] for h in here], states)
                         kept.append(states[0])
-                    out_ref[:, pl.ds(base, ROWS), :] = jnp.swapaxes(jnp.stack(kept), 0, 1)
+                    series[:, pl.ds(base, ROWS), :] = jnp.swapaxes(jnp.stack(kept), 0, 1)
                     return tuple(states)
 
                 states = lax.fori_loop(0, width // ROWS, scan, states)
+                save(c).start()
 
     for i in range(SWEEPS):
         own[i] = states[i]
@@ -188,54 +219,85 @@
             value = value + WRAP_WEIGHT * around[i][j : j + 1, :] * start[j]
         start[i] = value / (1.0 - WRAP_WEIGHT * around[i][i : i + 1, :])
     for e in range(plane):
-        value = out_ref[e]
         for i in range(SWEEPS):
-            value = value + table[i] * start[i][e : e + 1, :]
-        out_ref[e] = value
-
+            start_ref[e, i : i + 1, :] = start[i][e : e + 1, :]
+
+    save_table.wait()
+    for c in range(CHUNKS):
+        save(c).wait()
     for j in range(moves):
         for c in range(CHUNKS):
             for d in range(2):
                 transfer(j, c, d).wait_send()
 
 
+def finish(series_ref, table_ref, start_ref, out_ref):
+    value = series_ref[0]
+    for i in range(SWEEPS):
+        value = value + table_ref[i] * start_ref[0, i : i + 1, :]
+    out_ref[0] = value
+
+
 def solution(mesh):
     tm_size, sp_size = mesh.shape["tm"], mesh.shape["space"]
 
     def per_device(right_side, blocks, neighbors, shift_rates):
         plane, steps, nodes = right_side.shape
         moves = SWEEPS - 1
-        sigma = STEP_SCALE * shift_rates
-        coef = jnp.concatenate([1.0 / (1.0 + sigma), sigma - STEP_SCALE * DIAG_WEIGHT])
-        whole = pltpu.VMEM((plane, steps, nodes), jnp.float32)
-        piece = pltpu.VMEM((plane, steps // CHUNKS, nodes), jnp.float32)
+        f32 = jnp.float32
+        whole = pltpu.VMEM((plane, steps, nodes), f32)
+        pieces = [pltpu.VMEM((plane, width, nodes), f32) for _, width in windows(steps)]
         dma = pltpu.SemaphoreType.DMA
-        return pl.pallas_call(
+        series, table, start = pl.pallas_call(
             functools.partial(kernel, tm_size, sp_size),
-            out_shape=jax.ShapeDtypeStruct(right_side.shape, jnp.float32),
+            out_shape=(
+                jax.ShapeDtypeStruct(right_side.shape, f32),
+                jax.ShapeDtypeStruct((SWEEPS, steps, nodes), f32),
+                jax.ShapeDtypeStruct((plane, SWEEPS, nodes), f32),
+            ),
             in_specs=[
-                pl.BlockSpec(memory_space=pltpu.VMEM),
-                pl.BlockSpec(memory_space=pltpu.VMEM),
+                pl.BlockSpec(memory_space=pl.ANY),
+                pl.BlockSpec(memory_space=pl.ANY),
                 pl.BlockSpec(memory_space=pltpu.SMEM),
                 pl.BlockSpec(memory_space=pltpu.SMEM),
             ],
-            out_specs=pl.BlockSpec(memory_space=pltpu.VMEM),
-            scratch_shapes=[whole] * moves
-            + [piece] * (2 * moves * CHUNKS)
+            out_specs=(
+                pl.BlockSpec(memory_space=pl.ANY),
+                pl.BlockSpec(memory_space=pl.ANY),
+                pl.BlockSpec(memory_space=pltpu.VMEM),
+            ),
+            scratch_shapes=[whole] * SWEEPS
+            + [piece for _ in range(moves) for piece in pieces for _ in range(2)]
             + [
+                whole,
+                pltpu.VMEM(blocks.shape, f32),
                 pltpu.VMEM((plane, SLOTS * nodes, 2 * nodes), jnp.bfloat16),
-                pltpu.VMEM((SWEEPS, steps, nodes), jnp.float32),
-                pltpu.VMEM((tm_size - 1, SWEEPS, plane, nodes), jnp.float32),
-                pltpu.VMEM((SWEEPS, plane, nodes), jnp.float32),
+                pltpu.VMEM((SWEEPS, steps, nodes), f32),
+                pltpu.VMEM((tm_size - 1, SWEEPS, plane, nodes), f32),
+                pltpu.VMEM((SWEEPS, plane, nodes), f32),
                 dma((moves, CHUNKS, 2)),
                 dma((moves, CHUNKS, 2)),
                 dma((tm_size - 1,)),
                 dma((tm_size - 1,)),
+                dma((2,)),
+                dma((CHUNKS + 1,)),
             ],
             compiler_params=pltpu.CompilerParams(
-                collective_id=0, has_side_effects=True, vmem_limit_bytes=56 * 2**20
+                collective_id=0, has_side_effects=True, vmem_limit_bytes=60 * 2**20
             ),
-        )(right_side, blocks, neighbors % plane, coef)
+        )(right_side, blocks, neighbors, shift_rates)
+        block = pl.BlockSpec((1, steps, nodes), lambda e: (e, 0, 0))
+        return pl.pallas_call(
+            finish,
+            grid=(plane,),
+            out_shape=jax.ShapeDtypeStruct(right_side.shape, f32),
+            in_specs=[
+                block,
+                pl.BlockSpec((SWEEPS, steps, nodes), lambda e: (0, 0, 0)),
+                pl.BlockSpec((1, SWEEPS, nodes), lambda e: (e, 0, 0)),
+            ],
+            out_specs=block,
+        )(series, table, start)
 
     return jax.shard_map(
         per_device,

time: 159 us -> 156 us (0.981)
  local copies, waits for them, and re-layouts: 3.06 us -> 0 us
  Pallas kernels: 153 us -> 156 us
  other arithmetic: 2.57 us -> 0 us
    unnamed x1 -> x0, local copies, waits for them, and re-layouts: 3.06 us -> none
    pallas_call x1 -> x2, Pallas kernels: 153 us -> 156 us  [the longest x1 150 us: per_device(): pl.pallas_call(functools.partial(kernel, tm_size, sp_size), out_shape=(ja...]
where the time goes in v2:
time: 156 us
  Pallas kernels  156 us (100%)
    pallas_call x1, Pallas kernels, per_device(): pl.pallas_call(functools.partial(kernel, tm_size, sp_size), out_shape=(ja...  150 us
    pallas_call x1, Pallas kernels, per_device(): pl.pallas_call(finish, grid=(plane,), out_shape=jax.ShapeDtypeStruct(righ...  6.24 us

profile of v2, /device:TPU:0, one launch (start us, length us, event | category | flops | bytes accessed | tf_op | source)
XLA Modules:
  0.0 156.1 jit_solution(12841934081411770259)
XLA Ops:
  0.0 149.8 %shard_map.46 = (f32[8,512,128]{2,1,0:T(8,128)}, f32[4,512,128]{2,1,0:T(8,128)}, f32[8,4,128]{2,1,0:T(4,128)}) custom-call(f32[8,512,128]{2,1,0:T(8,128)} %x_ref.1, f32[8,7,128,128]{3,2,1,0:T(8,128)} %blocks_ref.1, s32[8,7]{1,0:T(8,128)} %near_ref.1, f32[4]{0:T(128)} %shift_ref.1), custom_call_target="tpu_custom_call" | custom-call | tf_op jit(solution)/shard_map/pallas_call | solution.py:251
  149.8 6.2 %shard_map.47 = f32[8,512,128]{2,1,0:T(8,128)} custom-call(f32[8,512,128]{2,1,0:T(8,128)} %get-tuple-element.8.series_ref, f32[4,512,128]{2,1,0:T(8,128)} %get-tuple-element.9.table_ref, f32[8,4,128]{2,1,0:T(4,128)} %get-tuple-element.10.start_ref), custom_call_target="tpu_custom_call" | custom-call | tf_op jit(solution)/shard_map/pallas_call | solution.py:290

commit v3 on v2

--- a/solution.py
+++ b/solution.py
@@ -232,10 +232,19 @@
 
 
 def finish(series_ref, table_ref, start_ref, out_ref):
-    value = series_ref[0]
-    for i in range(SWEEPS):
-        value = value + table_ref[i] * start_ref[0, i : i + 1, :]
-    out_ref[0] = value
+    steps = series_ref.shape[1]
+
+    def some(g, _):
+        rows = pl.ds(pl.multiple_of(g * 4 * ROWS, 4 * ROWS), 4 * ROWS)
+        lines = [table_ref[i, rows, :] for i in range(SWEEPS)]
+        for e in range(series_ref.shape[0]):
+            value = series_ref[e, rows, :]
+            for i in range(SWEEPS):
+                value = value + lines[i] * start_ref[e, i : i + 1, :]
+            out_ref[e, rows, :] = value
+        return 0
+
+    lax.fori_loop(0, steps // (4 * ROWS), some, 0)
 
 
 def solution(mesh):
@@ -286,15 +295,15 @@
                 collective_id=0, has_side_effects=True, vmem_limit_bytes=60 * 2**20
             ),
         )(right_side, blocks, neighbors, shift_rates)
-        block = pl.BlockSpec((1, steps, nodes), lambda e: (e, 0, 0))
+        block = pl.BlockSpec((2, steps, nodes), lambda e: (e, 0, 0))
         return pl.pallas_call(
             finish,
-            grid=(plane,),
+            grid=(plane // 2,),
             out_shape=jax.ShapeDtypeStruct(right_side.shape, f32),
             in_specs=[
                 block,
                 pl.BlockSpec((SWEEPS, steps, nodes), lambda e: (0, 0, 0)),
-                pl.BlockSpec((1, SWEEPS, nodes), lambda e: (e, 0, 0)),
+                pl.BlockSpec((2, SWEEPS, nodes), lambda e: (e, 0, 0)),
             ],
             out_specs=block,
         )(series, table, start)

time: 156 us -> 155 us (level)
  no operation moved by 1% of the time
where the time goes in v3:
time: 155 us
  Pallas kernels  155 us (100%)
    pallas_call x1, Pallas kernels, per_device(): pl.pallas_call(functools.partial(kernel, tm_size, sp_size), out_shape=(ja...  150 us
    pallas_call x1, Pallas kernels, per_device(): pl.pallas_call(finish, grid=(plane // 2,), out_shape=jax.ShapeDtypeStruct...  4.7 us

profile of v3, /device:TPU:0, one launch (start us, length us, event | category | flops | bytes accessed | tf_op | source)
XLA Modules:
  0.0 154.5 jit_solution(510404248844929884)
XLA Ops:
  0.0 149.8 %shard_map.46 = (f32[8,512,128]{2,1,0:T(8,128)}, f32[4,512,128]{2,1,0:T(8,128)}, f32[8,4,128]{2,1,0:T(4,128)}) custom-call(f32[8,512,128]{2,1,0:T(8,128)} %x_ref.1, f32[8,7,128,128]{3,2,1,0:T(8,128)} %blocks_ref.1, s32[8,7]{1,0:T(8,128)} %near_ref.1, f32[4]{0:T(128)} %shift_ref.1), custom_call_target="tpu_custom_call" | custom-call | tf_op jit(solution)/shard_map/pallas_call | solution.py:260
  149.8 4.7 %shard_map.47 = f32[8,512,128]{2,1,0:T(8,128)} custom-call(f32[8,512,128]{2,1,0:T(8,128)} %get-tuple-element.8.series_ref, f32[4,512,128]{2,1,0:T(8,128)} %get-tuple-element.9.table_ref, f32[8,4,128]{2,1,0:T(4,128)} %get-tuple-element.10.start_ref), custom_call_target="tpu_custom_call" | custom-call | tf_op jit(solution)/shard_map/pallas_call | solution.py:299
